TPU v7x, 256 devices: a whole 4x4x8 slice. The times are simulated.
256 devices in a mesh: rows: 256 (over x, z, y, core).
Axes of the slice: x: 4, y: 4, z: 8, core: 2. Of those that a mesh axis runs over, the one named last changes fastest.
Arguments:
- points_t: float32 [64, 262144], P(None, 'rows'), may hold values from -6 to 6
- pivots: int32 [2, 256], replicated, may hold values from 0 to 262143, as said below
Outputs:
- factor: bfloat16 [262144, 512], P('rows')
- residual_diag: float32 [262144], P('rows')
Inputs may be any that keep to these rules, and one draw needn't show every extreme that they name: `pivots`: all 512 indices are different. In each block at most 3 indices fall in one device's points, rows k * 1024 to (k + 1) * 1024 - 1, and in each block some device holds exactly 3.
All inputs are finite; a program needn't handle non-finite values.
Results may differ from a plain program's by a relative error of at most 0.001.
Values sent between devices are 32-bit elements; how exact they have to be, the bound alone decides.
A program may use at most 64 MiB of HBM per device.

v0:
```python
import jax
import jax.numpy as jnp
from jax import lax
from jax.experimental import pallas as pl
from jax.experimental.pallas import tpu as pltpu
from jax.sharding import PartitionSpec as P

NX, NZ, NY, NC = 4, 8, 4, 2
CAP = 3
BIG = 1 << 24


def exchange_kernel(piv_ref, pts_ref, out_ref, zs, zr, bs, br, as_, ar, cs, cr):
    me = lax.axis_index("rows")
    core = lax.rem(me, NC)
    y = lax.rem(me // NC, NY)
    z = lax.rem(me // (NC * NY), NZ)
    x = me // (NC * NY * NZ)
    a = x + core * (y - x)
    b = y + core * (x - y)

    def device(a_, b_, z_, core_):
        x_ = a_ + core * (b_ - a_)
        y_ = b_ + core * (a_ - b_)
        return ((x_ * NZ + z_) * NY + y_) * NC + core_

    def z_peer(k):
        return device(a, b, lax.rem(z + k, NZ), core)

    def b_peer(k):
        return device(a, lax.rem(b + k, 4), z, core)

    def a_peer(k):
        return device(lax.rem(a + k, 4), b, z, core)

    sibling = device(a, b, z, 1 - core)
    peers = (
        [z_peer(k) for k in range(1, NZ)]
        + [b_peer(k) for k in range(1, 4)]
        + [a_peer(k) for k in range(1, 4)]
        + [sibling]
    )
    barrier = pltpu.get_barrier_semaphore()
    for peer in peers:
        pl.semaphore_signal(barrier, inc=1, device_id=(peer,), device_id_type=pl.DeviceIdType.MESH)

    rows_here = pts_ref.shape[1]
    local = piv_ref[...] - me * rows_here
    key = jnp.where((local >= 0) & (local < rows_here), local, BIG)
    floor = jnp.full((2, 1), -1, jnp.int32)
    lanes = lax.broadcasted_iota(jnp.int32, (2, rows_here), 1)
    picks = []
    for _ in range(CAP):
        floor = jnp.min(jnp.where(key > floor, key, BIG), axis=1, keepdims=True)
        picks.append(jnp.where(lanes == floor, 1.0, 0.0).astype(jnp.float32))
    pick = jnp.concatenate(
        [p[0:1] for p in picks] + [jnp.zeros((1, rows_here), jnp.float32)]
        + [p[1:2] for p in picks] + [jnp.zeros((1, rows_here), jnp.float32)],
        axis=0,
    )
    slots = lax.dot_general(
        pick,
        pts_ref[...],
        (((1,), (1,)), ((), ())),
        precision=lax.Precision.HIGHEST,
        preferred_element_type=jnp.float32,
    )
    mine = core * 128 + a * 32 + b * 8 + z
    both = jnp.concatenate([slots[0:4], slots[4:8]], axis=1)
    for s in range(CAP):
        out_ref[mine * CAP + s] = both[s : s + 1]
    pl.semaphore_wait(barrier, len(peers))

    def send(start, count, send_sem, recv_sem, peer):
        part = out_ref.at[pl.ds(start * CAP, count * CAP)]
        copy = pltpu.make_async_remote_copy(
            src_ref=part,
            dst_ref=part,
            send_sem=send_sem,
            recv_sem=recv_sem,
            device_id=(peer,),
            device_id_type=pl.DeviceIdType.MESH,
        )
        copy.start()
        return copy

    def arrived(start, count, send_sem, recv_sem, peer):
        part = out_ref.at[pl.ds(start * CAP, count * CAP)]
        pltpu.make_async_remote_copy(
            src_ref=part,
            dst_ref=part,
            send_sem=send_sem,
            recv_sem=recv_sem,
            device_id=(peer,),
            device_id_type=pl.DeviceIdType.MESH,
        ).wait_recv()

    out = []
    for k in range(1, NZ):
        out.append(send(mine, 1, zs.at[k - 1], zr.at[k - 1], z_peer(k)))
    for k in range(1, NZ):
        arrived(core * 128 + a * 32 + b * 8 + lax.rem(z + NZ - k, NZ), 1, zs.at[k - 1], zr.at[k - 1], z_peer(k))
    for k in range(1, 4):
        out.append(send(core * 128 + a * 32 + b * 8, 8, bs.at[k - 1], br.at[k - 1], b_peer(k)))
    for k in range(1, 4):
        arrived(core * 128 + a * 32 + lax.rem(b + 4 - k, 4) * 8, 8, bs.at[k - 1], br.at[k - 1], b_peer(k))
    for k in range(1, 4):
        out.append(send(core * 128 + a * 32, 32, as_.at[k - 1], ar.at[k - 1], a_peer(k)))
    out.append(send(core * 128 + a * 32, 32, cs.at[0], cr.at[0], sibling))
    for k in range(1, 4):
        from_a = lax.rem(a + 4 - k, 4)
        arrived(core * 128 + from_a * 32, 32, as_.at[k - 1], ar.at[k - 1], a_peer(k))
        out.append(send(core * 128 + from_a * 32, 32, cs.at[k], cr.at[k], sibling))
    for k in range(4):
        from_a = lax.rem(b + 4 - k, 4)
        arrived((1 - core) * 128 + from_a * 32, 32, cs.at[k], cr.at[k], sibling)
    for copy in out:
        copy.wait_send()


def exchange(points_t, pivots):
    return pl.pallas_call(
        exchange_kernel,
        out_shape=jax.ShapeDtypeStruct((256 * CAP, 1, 128), jnp.float32),
        in_specs=[pl.BlockSpec(memory_space=pltpu.VMEM)] * 2,
        out_specs=pl.BlockSpec(memory_space=pltpu.VMEM),
        scratch_shapes=[
            pltpu.SemaphoreType.DMA((7,)),
            pltpu.SemaphoreType.DMA((7,)),
            pltpu.SemaphoreType.DMA((3,)),
            pltpu.SemaphoreType.DMA((3,)),
            pltpu.SemaphoreType.DMA((3,)),
            pltpu.SemaphoreType.DMA((3,)),
            pltpu.SemaphoreType.DMA((4,)),
            pltpu.SemaphoreType.DMA((4,)),
        ],
        compiler_params=pltpu.CompilerParams(collective_id=0, has_side_effects=True),
        name="exchange",
    )(pivots, points_t)


def places(pivots, rows_here):
    owner = pivots // rows_here
    before = (owner[:, :, None] == owner[:, None, :]) & (pivots[:, None, :] < pivots[:, :, None])
    rank = jnp.sum(before.astype(jnp.int32), axis=2)
    core = owner % NC
    y = (owner // NC) % NY
    z = (owner // (NC * NY)) % NZ
    x = owner // (NC * NY * NZ)
    a = jnp.where(core == 0, x, y)
    b = jnp.where(core == 0, y, x)
    return (core * 128 + a * 32 + b * 8 + z) * CAP + rank


LANES = 128
HIGHEST = lax.Precision.HIGHEST


def nt(left, right):
    return lax.dot_general(left, right, (((1,), (1,)), ((), ())), precision=HIGHEST, preferred_element_type=jnp.float32)


def tn(left, right):
    return lax.dot_general(left, right, (((0,), (0,)), ((), ())), precision=HIGHEST, preferred_element_type=jnp.float32)


def spread(column):
    return jnp.broadcast_to(column, (8, LANES))


def factor_kernel(place_ref, g_ref, pts_ref, f_ref, r_ref, pv_ref, m_ref, s_ref, kx_ref, q_ref):
    dim, points = pts_ref.shape
    size = m_ref.shape[0]
    piv = size // 2
    wide = size // LANES
    scale = -1.0 / (1.65 * dim)

    for j in range(size):
        pv_ref[j : j + 1, :] = g_ref[place_ref[j]]
    pivots = jnp.concatenate([pv_ref[:piv, :dim], pv_ref[piv:, dim:]], axis=0)
    squared = pivots * pivots
    norm_row = nt(jnp.ones((8, dim), jnp.float32), squared)[0:1]
    norm_col = jnp.sum(squared, axis=1, keepdims=True)
    m_ref[...] = jnp.exp((norm_col + norm_row - 2.0 * nt(pivots, pivots)) * scale)

    pts = pts_ref[...].T
    norm_pts = jnp.sum(pts * pts, axis=1, keepdims=True)
    kx_ref[...] = jnp.exp((norm_pts + norm_row - 2.0 * nt(pts, pivots)) * scale)

    sub = lax.broadcasted_iota(jnp.int32, (8, LANES), 0)
    lane = lax.broadcasted_iota(jnp.int32, (8, LANES), 1)

    for blk in range(wide):
        start, end = blk * LANES, (blk + 1) * LANES
        for c0 in range(start, end, 8):
            off = c0 - start
            rows = [m_ref[c0 : c0 + 8, v * LANES : (v + 1) * LANES] for v in range(wide)]
            cols = [spread(rows[blk][:, off + k : off + k + 1]) for k in range(8)]
            own = (lane >= off) & (lane < off + 8)
            rows[blk] = jnp.where(own, jnp.where(lane - off == sub, 1.0, 0.0), rows[blk])
            kept = list(rows)
            diag = cols[0]
            for j in range(8):
                inv = spread((1.0 / cols[j])[j : j + 1])
                scaled = jnp.where(sub == j, 0.0, cols[j]) * inv
                if j:
                    diag = jnp.where(sub == j, cols[j], diag)
                    kept = [jnp.where(sub == j, r, s) for r, s in zip(rows, kept)]
                for k in range(j + 1, 8):
                    cols[k] = cols[k] - scaled * spread(cols[k][j : j + 1])
                rows = [r - scaled * spread(r[j : j + 1]) for r in rows]
            root = lax.rsqrt(diag)
            kept[blk] = jnp.where(lane < off + 8, kept[blk], 0.0)
            for v in range(wide):
                s_ref[c0 : c0 + 8, v * LANES : (v + 1) * LANES] = kept[v] * root
            inv = 1.0 / diag
            turned = [[spread((r * inv)[k : k + 1]) for k in range(8)] for r in rows]
            for r0 in range(c0 + 8, end, 8):
                old = [m_ref[r0 : r0 + 8, v * LANES : (v + 1) * LANES] for v in range(wide)]
                factors = [spread(old[blk][:, off + k : off + k + 1]) for k in range(8)]
                old[blk] = jnp.where(own, 0.0, old[blk])
                for v in range(wide):
                    new = old[v]
                    for k in range(8):
                        new = new - factors[k] * turned[v][k]
                    m_ref[r0 : r0 + 8, v * LANES : (v + 1) * LANES] = new
        if end < size:
            update = tn(s_ref[start:end, end:], s_ref[start:end, :])
            for v in range(wide):
                part = slice(v * LANES, (v + 1) * LANES)
                if v == blk:
                    m_ref[end:, part] = -update[:, part]
                else:
                    m_ref[end:, part] = m_ref[end:, part] - update[:, part]
        new = nt(kx_ref[:, :end], s_ref[start:end, :end])
        f_ref[:, start:end] = new.astype(jnp.bfloat16)
        q_ref[...] = new * new if blk == 0 else q_ref[...] + new * new
    r_ref[...] = 1.0 - nt(jnp.ones((8, LANES), jnp.float32), q_ref[...])[0:1]


def factor_call(place, gathered, points_t, size=512):
    dim, points = points_t.shape
    return pl.pallas_call(
        factor_kernel,
        out_shape=[
            jax.ShapeDtypeStruct((points, size), jnp.bfloat16),
            jax.ShapeDtypeStruct((1, points), jnp.float32),
        ],
        in_specs=[
            pl.BlockSpec(memory_space=pltpu.SMEM),
            pl.BlockSpec(memory_space=pltpu.VMEM),
            pl.BlockSpec(memory_space=pltpu.VMEM),
        ],
        out_specs=[pl.BlockSpec(memory_space=pltpu.VMEM)] * 2,
        scratch_shapes=[
            pltpu.VMEM((size, LANES), jnp.float32),
            pltpu.VMEM((size, size), jnp.float32),
            pltpu.VMEM((size, size), jnp.float32),
            pltpu.VMEM((points, size), jnp.float32),
            pltpu.VMEM((points, LANES), jnp.float32),
        ],
        compiler_params=pltpu.CompilerParams(vmem_limit_bytes=40 << 20),
        name="factor",
    )(place, gathered, points_t)


def body(points_t, pivots):
    place = places(pivots, points_t.shape[1]).reshape(-1)
    factor, resid = factor_call(place, exchange(points_t, pivots), points_t)
    return (factor, resid.reshape(-1))


def solution(mesh):
    return jax.shard_map(
        body,
        mesh=mesh,
        in_specs=(P(None, "rows"), P()),
        out_specs=(P("rows", None), P("rows")),
        check_vma=False,
    )
```

profile of v0, /device:TPU:1, one launch (start us, length us, event | category | flops | bytes accessed | tf_op | source)
XLA Modules:
  0.0 56.9 jit_solution(2468156451250997655)
XLA Ops:
  0.6 0.0 copy-start.2
  0.6 0.8 %and_select_fusion.6 = s32[2,256]{1,0:T(2,128)S(1)} fusion(s32[2,256]{1,0:T(2,128)} %piv_ref.1), kind=kLoop, calls=%fused_computation.11 | loop fusion | flops 7680 | bytes 4096 | tf_op jit(solution)/shard_map/jit(floor_divide)/jit(_where)/select_n | solution.py:143
  1.4 0.0 copy-done.2
  1.4 0.3 convert_reduce_fusion
  1.8 0.0 copy-start.1
  1.8 25.8 %exchange.1.g_ref = f32[768,1,128]{2,1,0:T(1,128)} custom-call(s32[2,256]{1,0:T(2,128)} %piv_ref.1, f32[64,1024]{1,0:T(8,128)} %pts_ref.3), custom_call_target="tpu_custom_call" | custom-call | tf_op jit(solution)/shard_map/exchange/pallas_call | solution.py:122
  27.6 0.0 copy-done.1
  27.6 0.0 copy-start
  27.6 1.0 %copy-done = f32[768,1,128]{2,1,0:T(1,128)S(1)} copy-done((f32[768,1,128]{2,1,0:T(1,128)S(1)}, f32[768,1,128]{2,1,0:T(1,128)}, u32[]{:S(2)}) %copy-start) | copy-done | bytes 393240
  28.6 28.3 %factor.1 = (bf16[1024,512]{1,0:T(8,128)(2,1)}, f32[1,1024]{1,0:T(1,128)}) custom-call(s32[512]{0:T(512)S(1)} %bitcast.4, f32[768,1,128]{2,1,0:T(1,128)S(1)} %copy-done, f32[64,1024]{1,0:T(8,128)S(1)} %copy-done.1), custom_call_target="tpu_custom_call" | custom-call | tf_op jit(solution)/shard_map/factor/pallas_call | solution.py:243
  (2 shorter events, 0.0 us)
Async XLA Ops:
  0.6 0.8 %copy-start.2 = (s32[2,256]{1,0:T(2,128)S(1)}, s32[2,256]{1,0:T(2,128)}, u32[]{:S(2)}) copy-start(s32[2,256]{1,0:T(2,128)} %piv_ref.1) | copy-start | bytes 6148
  1.8 25.8 %copy-start.1 = (f32[64,1024]{1,0:T(8,128)S(1)}, f32[64,1024]{1,0:T(8,128)}, u32[]{:S(2)}) copy-start(f32[64,1024]{1,0:T(8,128)} %pts_ref.3) | copy-start | bytes 786436
  27.6 1.0 %copy-start = (f32[768,1,128]{2,1,0:T(1,128)S(1)}, f32[768,1,128]{2,1,0:T(1,128)}, u32[]{:S(2)}) copy-start(f32[768,1,128]{2,1,0:T(1,128)} %exchange.1.g_ref) | copy-start | bytes 1179652
where the time goes:
time: 57.1 us; the launch traced here: 56.9 us
  Pallas kernels  54.1 us (95%)
  other arithmetic  1.11 us (2%)
  local copies, waits for them, and re-layouts  1 us (2%)
  between operations  0.69 us (1%)
    pallas_call x1, Pallas kernels, factor_call(): pl.pallas_call(factor_kernel, out_shape=[jax.ShapeDtypeStruct((points, si...  28.3 us
    pallas_call x1, Pallas kernels, exchange(): pl.pallas_call(exchange_kernel, out_shape=jax.ShapeDtypeStruct((256 * CAP...  25.8 us

commit v1 on v0

--- a/solution.py
+++ b/solution.py
@@ -7,45 +7,42 @@
 
 NX, NZ, NY, NC = 4, 8, 4, 2
 CAP = 3
+NEAR = 5
+HALF = NX * NY * NZ * CAP
+FAR_AT = NX * NY * NEAR * CAP
 BIG = 1 << 24
-
-
-def exchange_kernel(piv_ref, pts_ref, out_ref, zs, zr, bs, br, as_, ar, cs, cr):
+MESH = pl.DeviceIdType.MESH
+
+
+def exchange_kernel(piv_ref, pts_hbm, out_ref, place_ref, pts_ref, pts_sem, zs, zr, ps, pr, cs, cr):
     me = lax.axis_index("rows")
     core = lax.rem(me, NC)
     y = lax.rem(me // NC, NY)
     z = lax.rem(me // (NC * NY), NZ)
     x = me // (NC * NY * NZ)
-    a = x + core * (y - x)
-    b = y + core * (x - y)
-
-    def device(a_, b_, z_, core_):
-        x_ = a_ + core * (b_ - a_)
-        y_ = b_ + core * (a_ - b_)
+
+    def device(x_, y_, z_, core_):
         return ((x_ * NZ + z_) * NY + y_) * NC + core_
 
     def z_peer(k):
-        return device(a, b, lax.rem(z + k, NZ), core)
-
-    def b_peer(k):
-        return device(a, lax.rem(b + k, 4), z, core)
-
-    def a_peer(k):
-        return device(lax.rem(a + k, 4), b, z, core)
-
-    sibling = device(a, b, z, 1 - core)
-    peers = (
-        [z_peer(k) for k in range(1, NZ)]
-        + [b_peer(k) for k in range(1, 4)]
-        + [a_peer(k) for k in range(1, 4)]
-        + [sibling]
-    )
+        return device(x, y, lax.rem(z + k, NZ), core)
+
+    flat = [(i, k) for i in range(NX) for k in range(NY) if i or k]
+
+    def plane_peer(i, k):
+        return device(lax.rem(x + i, NX), lax.rem(y + k, NY), z, core)
+
+    sibling = device(x, y, z, 1 - core)
+    peers = [z_peer(k) for k in range(1, NZ)] + [plane_peer(i, k) for i, k in flat] + [sibling]
     barrier = pltpu.get_barrier_semaphore()
     for peer in peers:
-        pl.semaphore_signal(barrier, inc=1, device_id=(peer,), device_id_type=pl.DeviceIdType.MESH)
+        pl.semaphore_signal(barrier, inc=1, device_id=(peer,), device_id_type=MESH)
+    load = pltpu.make_async_copy(pts_hbm, pts_ref, pts_sem)
+    load.start()
 
     rows_here = pts_ref.shape[1]
-    local = piv_ref[...] - me * rows_here
+    pivots = piv_ref[...]
+    local = pivots - me * rows_here
     key = jnp.where((local >= 0) & (local < rows_here), local, BIG)
     floor = jnp.full((2, 1), -1, jnp.int32)
     lanes = lax.broadcasted_iota(jnp.int32, (2, rows_here), 1)
@@ -53,11 +50,9 @@
     for _ in range(CAP):
         floor = jnp.min(jnp.where(key > floor, key, BIG), axis=1, keepdims=True)
         picks.append(jnp.where(lanes == floor, 1.0, 0.0).astype(jnp.float32))
-    pick = jnp.concatenate(
-        [p[0:1] for p in picks] + [jnp.zeros((1, rows_here), jnp.float32)]
-        + [p[1:2] for p in picks] + [jnp.zeros((1, rows_here), jnp.float32)],
-        axis=0,
-    )
+    pad = jnp.zeros((1, rows_here), jnp.float32)
+    pick = jnp.concatenate([p[0:1] for p in picks] + [pad] + [p[1:2] for p in picks] + [pad], axis=0)
+    load.wait()
     slots = lax.dot_general(
         pick,
         pts_ref[...],
@@ -65,91 +60,120 @@
         precision=lax.Precision.HIGHEST,
         preferred_element_type=jnp.float32,
     )
-    mine = core * 128 + a * 32 + b * 8 + z
     both = jnp.concatenate([slots[0:4], slots[4:8]], axis=1)
+
+    def near_at(core_, plane):
+        return core_ * HALF + plane * (NEAR * CAP)
+
+    def far_at(core_, plane):
+        return core_ * HALF + FAR_AT + plane * ((NZ - NEAR) * CAP)
+
+    def chunk_at(core_, plane, step):
+        zz = (step + 2) % NZ
+        if zz < NEAR:
+            return near_at(core_, plane) + zz * CAP
+        return far_at(core_, plane) + (zz - NEAR) * CAP
+
+    here = x * NY + y
+    mine = chunk_at(core, here, 0)
     for s in range(CAP):
-        out_ref[mine * CAP + s] = both[s : s + 1]
+        out_ref[mine + s] = both[s : s + 1]
     pl.semaphore_wait(barrier, len(peers))
 
-    def send(start, count, send_sem, recv_sem, peer):
-        part = out_ref.at[pl.ds(start * CAP, count * CAP)]
-        copy = pltpu.make_async_remote_copy(
-            src_ref=part,
-            dst_ref=part,
+    def remote(src, dst, count, send_sem, recv_sem, peer):
+        return pltpu.make_async_remote_copy(
+            src_ref=out_ref.at[pl.ds(src, count)],
+            dst_ref=out_ref.at[pl.ds(dst, count)],
             send_sem=send_sem,
             recv_sem=recv_sem,
             device_id=(peer,),
-            device_id_type=pl.DeviceIdType.MESH,
+            device_id_type=MESH,
         )
+
+    sent = []
+
+    def send(*what):
+        copy = remote(*what)
         copy.start()
-        return copy
-
-    def arrived(start, count, send_sem, recv_sem, peer):
-        part = out_ref.at[pl.ds(start * CAP, count * CAP)]
-        pltpu.make_async_remote_copy(
-            src_ref=part,
-            dst_ref=part,
-            send_sem=send_sem,
-            recv_sem=recv_sem,
-            device_id=(peer,),
-            device_id_type=pl.DeviceIdType.MESH,
+        sent.append(copy)
+
+    near_steps = [1, NZ - 1, 2, NZ - 2]
+    far_steps = [k for k in range(1, NZ) if k not in near_steps]
+    for k in far_steps + near_steps:
+        send(mine, chunk_at(core, here, -k), CAP, zs.at[k - 1], zr.at[k - 1], z_peer(k))
+
+    as_float = jnp.concatenate([pivots, jnp.zeros((6, pivots.shape[1]), jnp.int32)], axis=0).astype(jnp.float32)
+    columns = jnp.transpose(as_float)
+    ranks = []
+    for block in range(2):
+        other = columns[:, block : block + 1]
+        row = as_float[block : block + 1]
+        first = ((pivots[block : block + 1] // rows_here) * rows_here).astype(jnp.float32)
+        before = (other < row) & (other >= first)
+        ranks.append(jnp.sum(jnp.where(before, 1.0, 0.0), axis=0, keepdims=True))
+    rank = jnp.concatenate(ranks, axis=0).astype(jnp.int32)
+    owner = pivots // rows_here
+    o_core = lax.rem(owner, NC)
+    o_y = lax.rem(owner // NC, NY)
+    o_z = lax.rem(owner // (NC * NY), NZ)
+    o_x = owner // (NC * NY * NZ)
+    o_plane = o_x * NY + o_y
+    zz = lax.rem(o_z - z + (NZ + 2), NZ)
+    place_ref[...] = (
+        jnp.where(
+            zz < NEAR,
+            near_at(o_core, o_plane) + zz * CAP,
+            far_at(o_core, o_plane) + (zz - NEAR) * CAP,
+        )
+        + rank
+    )
+
+    def z_arrived(k):
+        remote(mine, chunk_at(core, here, -k), CAP, zs.at[k - 1], zr.at[k - 1], z_peer(k)).wait_recv()
+
+    for group, steps, at, count in (
+        (0, near_steps, near_at, NEAR * CAP),
+        (1, far_steps, far_at, (NZ - NEAR) * CAP),
+    ):
+        for k in steps:
+            z_arrived(k)
+        for n, (i, k) in enumerate(flat):
+            send(at(core, here), at(core, here), count, ps.at[group, n], pr.at[group, n], plane_peer(i, k))
+    for group, at, count in ((0, near_at, NEAR * CAP), (1, far_at, (NZ - NEAR) * CAP)):
+        for n, (i, k) in enumerate(flat):
+            source = lax.rem(x + NX - i, NX) * NY + lax.rem(y + NY - k, NY)
+            remote(at(core, source), at(core, source), count, ps.at[group, n], pr.at[group, n], plane_peer(i, k)).wait_recv()
+        send(at(core, 0), at(core, 0), count * NX * NY, cs.at[group], cr.at[group], sibling)
+    for group, at, count in ((0, near_at, NEAR * CAP), (1, far_at, (NZ - NEAR) * CAP)):
+        remote(
+            at(1 - core, 0), at(1 - core, 0), count * NX * NY, cs.at[group], cr.at[group], sibling
         ).wait_recv()
-
-    out = []
-    for k in range(1, NZ):
-        out.append(send(mine, 1, zs.at[k - 1], zr.at[k - 1], z_peer(k)))
-    for k in range(1, NZ):
-        arrived(core * 128 + a * 32 + b * 8 + lax.rem(z + NZ - k, NZ), 1, zs.at[k - 1], zr.at[k - 1], z_peer(k))
-    for k in range(1, 4):
-        out.append(send(core * 128 + a * 32 + b * 8, 8, bs.at[k - 1], br.at[k - 1], b_peer(k)))
-    for k in range(1, 4):
-        arrived(core * 128 + a * 32 + lax.rem(b + 4 - k, 4) * 8, 8, bs.at[k - 1], br.at[k - 1], b_peer(k))
-    for k in range(1, 4):
-        out.append(send(core * 128 + a * 32, 32, as_.at[k - 1], ar.at[k - 1], a_peer(k)))
-    out.append(send(core * 128 + a * 32, 32, cs.at[0], cr.at[0], sibling))
-    for k in range(1, 4):
-        from_a = lax.rem(a + 4 - k, 4)
-        arrived(core * 128 + from_a * 32, 32, as_.at[k - 1], ar.at[k - 1], a_peer(k))
-        out.append(send(core * 128 + from_a * 32, 32, cs.at[k], cr.at[k], sibling))
-    for k in range(4):
-        from_a = lax.rem(b + 4 - k, 4)
-        arrived((1 - core) * 128 + from_a * 32, 32, cs.at[k], cr.at[k], sibling)
-    for copy in out:
+    for copy in sent:
         copy.wait_send()
 
 
 def exchange(points_t, pivots):
     return pl.pallas_call(
         exchange_kernel,
-        out_shape=jax.ShapeDtypeStruct((256 * CAP, 1, 128), jnp.float32),
-        in_specs=[pl.BlockSpec(memory_space=pltpu.VMEM)] * 2,
-        out_specs=pl.BlockSpec(memory_space=pltpu.VMEM),
+        out_shape=[
+            pltpu.VMEM((NC * HALF, 1, 128), jnp.float32),
+            pltpu.VMEM(pivots.shape, jnp.int32),
+        ],
+        in_specs=[pl.BlockSpec(memory_space=pltpu.VMEM), pl.BlockSpec(memory_space=pl.ANY)],
+        out_specs=[pl.BlockSpec(memory_space=pltpu.VMEM)] * 2,
         scratch_shapes=[
-            pltpu.SemaphoreType.DMA((7,)),
-            pltpu.SemaphoreType.DMA((7,)),
-            pltpu.SemaphoreType.DMA((3,)),
-            pltpu.SemaphoreType.DMA((3,)),
-            pltpu.SemaphoreType.DMA((3,)),
-            pltpu.SemaphoreType.DMA((3,)),
-            pltpu.SemaphoreType.DMA((4,)),
-            pltpu.SemaphoreType.DMA((4,)),
+            pltpu.VMEM(points_t.shape, jnp.float32),
+            pltpu.SemaphoreType.DMA(()),
+            pltpu.SemaphoreType.DMA((NZ - 1,)),
+            pltpu.SemaphoreType.DMA((NZ - 1,)),
+            pltpu.SemaphoreType.DMA((2, NX * NY - 1)),
+            pltpu.SemaphoreType.DMA((2, NX * NY - 1)),
+            pltpu.SemaphoreType.DMA((2,)),
+            pltpu.SemaphoreType.DMA((2,)),
         ],
         compiler_params=pltpu.CompilerParams(collective_id=0, has_side_effects=True),
         name="exchange",
     )(pivots, points_t)
-
-
-def places(pivots, rows_here):
-    owner = pivots // rows_here
-    before = (owner[:, :, None] == owner[:, None, :]) & (pivots[:, None, :] < pivots[:, :, None])
-    rank = jnp.sum(before.astype(jnp.int32), axis=2)
-    core = owner % NC
-    y = (owner // NC) % NY
-    z = (owner // (NC * NY)) % NZ
-    x = owner // (NC * NY * NZ)
-    a = jnp.where(core == 0, x, y)
-    b = jnp.where(core == 0, y, x)
-    return (core * 128 + a * 32 + b * 8 + z) * CAP + rank
 
 
 LANES = 128
@@ -176,7 +200,7 @@
     scale = -1.0 / (1.65 * dim)
 
     for j in range(size):
-        pv_ref[j : j + 1, :] = g_ref[place_ref[j]]
+        pv_ref[j : j + 1, :] = g_ref[place_ref[j // piv, j % piv]]
     pivots = jnp.concatenate([pv_ref[:piv, :dim], pv_ref[piv:, dim:]], axis=0)
     squared = pivots * pivots
     norm_row = nt(jnp.ones((8, dim), jnp.float32), squared)[0:1]
@@ -265,8 +289,8 @@
 
 
 def body(points_t, pivots):
-    place = places(pivots, points_t.shape[1]).reshape(-1)
-    factor, resid = factor_call(place, exchange(points_t, pivots), points_t)
+    gathered, place = exchange(points_t, pivots)
+    factor, resid = factor_call(place, gathered, points_t)
     return (factor, resid.reshape(-1))
 
 

time: 57.1 us -> 51.4 us (0.900)
  Pallas kernels: 54.1 us -> 50.6 us
  other arithmetic: 1.11 us -> 0 us
  local copies, waits for them, and re-layouts: 1 us -> 0.01 us
    pallas_call x1, Pallas kernels: 25.8 us -> 22.3 us  [exchange(): pl.pallas_call(exchange_kernel, out_shape=[pltpu.VMEM((NC * HALF, 1, 128)...]
    unnamed x7 -> x2, local copies, waits for them, and re-layouts: 1 us -> 0.01 us
    select_n x1 -> x0, other arithmetic: 0.75 us -> none  [places(): owner = pivots // rows_here]
where the time goes in v1:
time: 51.4 us; the launch traced here: 51.3 us
  Pallas kernels  50.6 us (98%)
  between operations  0.65 us (1%)
    pallas_call x1, Pallas kernels, factor_call(): pl.pallas_call(factor_kernel, out_shape=[jax.ShapeDtypeStruct((points, si...  28.3 us
    pallas_call x1, Pallas kernels, exchange(): pl.pallas_call(exchange_kernel, out_shape=[pltpu.VMEM((NC * HALF, 1, 128)...  22.3 us

profile of v1, /device:TPU:1, one launch (start us, length us, event | category | flops | bytes accessed | tf_op | source)
XLA Modules:
  0.0 51.3 jit_solution(6588053859503430173)
XLA Ops:
  0.6 0.0 copy-start
  0.6 22.3 %exchange.1 = (f32[768,1,128]{2,1,0:T(1,128)S(1)}, s32[2,256]{1,0:T(2,128)S(1)}) custom-call(s32[2,256]{1,0:T(2,128)} %piv_ref.1, f32[64,1024]{1,0:T(8,128)} %pts_ref.1), custom_call_target="tpu_custom_call" | custom-call | tf_op jit(solution)/shard_map/exchange/pallas_call | solution.py:156
  23.0 0.0 copy-done
  23.0 28.3 %factor.1 = (bf16[1024,512]{1,0:T(8,128)(2,1)}, f32[1,1024]{1,0:T(1,128)}) custom-call(s32[2,256]{1,0:T(2,128)S(1)} %get-tuple-element.6.place_ref, f32[768,1,128]{2,1,0:T(1,128)S(1)} %get-tuple-element.7.g_ref, f32[64,1024]{1,0:T(8,128)S(1)} %copy-done), custom_call_target="tpu_custom_call" | custom-call | tf_op jit(solution)/shard_map/factor/pallas_call | solution.py:267
Async XLA Ops:
  0.6 22.3 %copy-start = (f32[64,1024]{1,0:T(8,128)S(1)}, f32[64,1024]{1,0:T(8,128)}, u32[]{:S(2)}) copy-start(f32[64,1024]{1,0:T(8,128)} %pts_ref.1) | copy-start | bytes 786436

commit v2 on v1

--- a/solution.py
+++ b/solution.py
@@ -178,21 +178,27 @@
 
 LANES = 128
 HIGHEST = lax.Precision.HIGHEST
-
-
-def nt(left, right):
-    return lax.dot_general(left, right, (((1,), (1,)), ((), ())), precision=HIGHEST, preferred_element_type=jnp.float32)
-
-
-def tn(left, right):
-    return lax.dot_general(left, right, (((0,), (0,)), ((), ())), precision=HIGHEST, preferred_element_type=jnp.float32)
+CHUNK = 256
+
+
+def nt(left, right, precision=HIGHEST):
+    return lax.dot_general(left, right, (((1,), (1,)), ((), ())), precision=precision, preferred_element_type=jnp.float32)
+
+
+def nn(left, right):
+    return lax.dot_general(left, right, (((1,), (0,)), ((), ())), precision=HIGHEST, preferred_element_type=jnp.float32)
 
 
 def spread(column):
     return jnp.broadcast_to(column, (8, LANES))
 
 
-def factor_kernel(place_ref, g_ref, pts_ref, f_ref, r_ref, pv_ref, m_ref, s_ref, kx_ref, q_ref):
+def halves(value):
+    high = value.astype(jnp.bfloat16)
+    return high, (value - high.astype(jnp.float32)).astype(jnp.bfloat16)
+
+
+def factor_kernel(place_ref, g_ref, pts_ref, f_ref, r_ref, pv_ref, m_ref, s_ref, l_ref, w_ref, kh_ref, kl_ref, g_last_ref, q_ref):
     dim, points = pts_ref.shape
     size = m_ref.shape[0]
     piv = size // 2
@@ -209,56 +215,143 @@
 
     pts = pts_ref[...].T
     norm_pts = jnp.sum(pts * pts, axis=1, keepdims=True)
-    kx_ref[...] = jnp.exp((norm_pts + norm_row - 2.0 * nt(pts, pivots)) * scale)
+    kx = jnp.exp((norm_pts + norm_row - 2.0 * nt(pts, pivots)) * scale)
+    g_last_ref[...] = kx[:, size - LANES :]
+    kh, kl = halves(kx)
+    kh_ref[...] = kh
+    kl_ref[...] = kl
 
     sub = lax.broadcasted_iota(jnp.int32, (8, LANES), 0)
     lane = lax.broadcasted_iota(jnp.int32, (8, LANES), 1)
 
-    for blk in range(wide):
-        start, end = blk * LANES, (blk + 1) * LANES
-        for c0 in range(start, end, 8):
-            off = c0 - start
-            rows = [m_ref[c0 : c0 + 8, v * LANES : (v + 1) * LANES] for v in range(wide)]
-            cols = [spread(rows[blk][:, off + k : off + k + 1]) for k in range(8)]
+    def lanes(v):
+        return slice(v * LANES, (v + 1) * LANES)
+
+    trail = []
+    bulk = []
+
+    def pump(queue, count):
+        for _ in range(min(count, len(queue))):
+            queue.pop(0)()
+
+    def diagonal(blk):
+        start = blk * LANES
+        part = [m_ref[start + 8 * g : start + 8 * g + 8, lanes(blk)] for g in range(LANES // 8)]
+
+        def update(g, off, own, turned):
+            factors = [spread(part[g][:, off + k : off + k + 1]) for k in range(8)]
+            new = jnp.where(own, 0.0, part[g])
+            for k in range(8):
+                new = new - factors[k] * turned[k]
+            part[g] = new
+
+        for g in range(len(part)):
+            off = 8 * g
+            rows = part[g]
+            cols = [spread(rows[:, off + k : off + k + 1]) for k in range(8)]
             own = (lane >= off) & (lane < off + 8)
-            rows[blk] = jnp.where(own, jnp.where(lane - off == sub, 1.0, 0.0), rows[blk])
-            kept = list(rows)
+            rows = jnp.where(own, jnp.where(lane - off == sub, 1.0, 0.0), rows)
+            kept = rows
             diag = cols[0]
+            share = -(-len(trail) // 7)
+            bulk_share = -(-len(bulk) // ((len(part) - g) * 4))
             for j in range(8):
                 inv = spread((1.0 / cols[j])[j : j + 1])
                 scaled = jnp.where(sub == j, 0.0, cols[j]) * inv
                 if j:
                     diag = jnp.where(sub == j, cols[j], diag)
-                    kept = [jnp.where(sub == j, r, s) for r, s in zip(rows, kept)]
+                    kept = jnp.where(sub == j, rows, kept)
                 for k in range(j + 1, 8):
                     cols[k] = cols[k] - scaled * spread(cols[k][j : j + 1])
-                rows = [r - scaled * spread(r[j : j + 1]) for r in rows]
-            root = lax.rsqrt(diag)
-            kept[blk] = jnp.where(lane < off + 8, kept[blk], 0.0)
-            for v in range(wide):
-                s_ref[c0 : c0 + 8, v * LANES : (v + 1) * LANES] = kept[v] * root
-            inv = 1.0 / diag
-            turned = [[spread((r * inv)[k : k + 1]) for k in range(8)] for r in rows]
-            for r0 in range(c0 + 8, end, 8):
-                old = [m_ref[r0 : r0 + 8, v * LANES : (v + 1) * LANES] for v in range(wide)]
-                factors = [spread(old[blk][:, off + k : off + k + 1]) for k in range(8)]
-                old[blk] = jnp.where(own, 0.0, old[blk])
-                for v in range(wide):
-                    new = old[v]
-                    for k in range(8):
-                        new = new - factors[k] * turned[v][k]
-                    m_ref[r0 : r0 + 8, v * LANES : (v + 1) * LANES] = new
-        if end < size:
-            update = tn(s_ref[start:end, end:], s_ref[start:end, :])
-            for v in range(wide):
-                part = slice(v * LANES, (v + 1) * LANES)
-                if v == blk:
-                    m_ref[end:, part] = -update[:, part]
-                else:
-                    m_ref[end:, part] = m_ref[end:, part] - update[:, part]
-        new = nt(kx_ref[:, :end], s_ref[start:end, :end])
-        f_ref[:, start:end] = new.astype(jnp.bfloat16)
-        q_ref[...] = new * new if blk == 0 else q_ref[...] + new * new
+                rows = rows - scaled * spread(rows[j : j + 1])
+                pump(trail, share)
+                if j % 2:
+                    pump(bulk, bulk_share)
+            pump(trail, len(trail))
+            rows = rows * (1.0 / diag)
+            turned = [spread(rows[k : k + 1]) for k in range(8)]
+            kept = jnp.where(lane < off + 8, kept, 0.0) * lax.rsqrt(diag)
+            s_ref[start + off : start + off + 8, lanes(blk)] = kept
+            if g + 1 < len(part):
+                update(g + 1, off, own, turned)
+            for h in range(g + 2, len(part)):
+                trail.append(lambda h=h, off=off, own=own, turned=turned: update(h, off, own, turned))
+        pump(bulk, len(bulk))
+
+    def block(ref, r, c):
+        return ref[r * LANES : (r + 1) * LANES, lanes(c)]
+
+    def put_upper(blk, c):
+        s_ref[blk * LANES : (blk + 1) * LANES, lanes(c)] = nn(block(s_ref, blk, blk), block(m_ref, blk, c))
+
+    def put_lower(blk, r):
+        l_ref[r * LANES : (r + 1) * LANES, :] = nt(block(m_ref, r, blk), block(s_ref, blk, blk))
+
+    def put_outer(blk, r, c):
+        change = nn(l_ref[r * LANES : (r + 1) * LANES, :], block(s_ref, blk, c))
+        old = 0.0 if c == blk else block(m_ref, r, c)
+        m_ref[r * LANES : (r + 1) * LANES, lanes(c)] = old - change
+
+    def finish(new, part, c):
+        f_ref[part, lanes(c)] = new.astype(jnp.bfloat16)
+        q_ref[part, :] = new * new if c == 0 else q_ref[part, :] + new * new
+
+    def product(left_high, left_low, weights):
+        both = nt(left_high, weights, None) + nt(left_low, weights, None)
+        return both[:, :LANES] + both[:, LANES:]
+
+    def put_factor(blk, r0):
+        part = slice(r0, r0 + CHUNK)
+        width = (blk + 1) * LANES
+        weights = w_ref[blk % 2, :, :width]
+        finish(product(kh_ref[part, :width], kl_ref[part, :width], weights), part, blk)
+
+    def put_weights(blk, value):
+        high, low = halves(value)
+        w_ref[blk % 2, :LANES, : value.shape[1]] = high
+        w_ref[blk % 2, LANES:, : value.shape[1]] = low
+
+    last = wide - 1
+
+    def put_rest(r0):
+        part = slice(r0, r0 + CHUNK)
+        width = last * LANES
+        new = product(kh_ref[part, :width], kl_ref[part, :width], w_ref[last % 2, :, :width])
+        high, low = halves(g_last_ref[part, :] + new)
+        kh_ref[part, lanes(last)] = high
+        kl_ref[part, lanes(last)] = low
+
+    for blk in range(wide):
+        diagonal(blk)
+        if blk == last:
+            break
+        put_upper(blk, blk + 1)
+        put_lower(blk, blk + 1)
+        put_outer(blk, blk + 1, blk + 1)
+
+        def later(blk=blk):
+            others = [c for c in range(wide) if c not in (blk, blk + 1)]
+            for c in others:
+                bulk.append(lambda c=c: put_upper(blk, c))
+            for c in others + [blk]:
+                bulk.append(lambda c=c: put_outer(blk, blk + 1, c))
+            for r in range(blk + 2, wide):
+                bulk.append(lambda r=r: put_lower(blk, r))
+                for c in range(wide):
+                    bulk.append(lambda r=r, c=c: put_outer(blk, r, c))
+            if blk + 1 == last:
+                bulk.append(lambda: put_weights(last, m_ref[last * LANES :, : last * LANES]))
+                for r0 in range(0, points, CHUNK):
+                    bulk.append(lambda r0=r0: put_rest(r0))
+            bulk.append(lambda: put_weights(blk, s_ref[blk * LANES : (blk + 1) * LANES, : (blk + 1) * LANES]))
+            for r0 in range(0, points, CHUNK):
+                bulk.append(lambda r0=r0: put_factor(blk, r0))
+
+        later()
+    tail = jnp.concatenate(halves(block(s_ref, last, last)), axis=0)
+    for r0 in range(0, points, CHUNK):
+        part = slice(r0, r0 + CHUNK)
+        finish(product(kh_ref[part, lanes(last)], kl_ref[part, lanes(last)], tail), part, last)
     r_ref[...] = 1.0 - nt(jnp.ones((8, LANES), jnp.float32), q_ref[...])[0:1]
 
 
@@ -280,7 +373,11 @@
             pltpu.VMEM((size, LANES), jnp.float32),
             pltpu.VMEM((size, size), jnp.float32),
             pltpu.VMEM((size, size), jnp.float32),
-            pltpu.VMEM((points, size), jnp.float32),
+            pltpu.VMEM((size, LANES), jnp.float32),
+            pltpu.VMEM((2, 2 * LANES, size), jnp.bfloat16),
+            pltpu.VMEM((points, size), jnp.bfloat16),
+            pltpu.VMEM((points, size), jnp.bfloat16),
+            pltpu.VMEM((points, LANES), jnp.float32),
             pltpu.VMEM((points, LANES), jnp.float32),
         ],
         compiler_params=pltpu.CompilerParams(vmem_limit_bytes=40 << 20),

time: 51.4 us -> 45.5 us (0.89)
  Pallas kernels: 50.6 us -> 44.7 us
    pallas_call x1, Pallas kernels: 28.3 us -> 22.4 us  [factor_call(): pl.pallas_call(factor_kernel, out_shape=[jax.ShapeDtypeStruct((points, si...]
where the time goes in v2:
time: 45.5 us; the launch traced here: 45.4 us
  Pallas kernels  44.7 us (98%)
  between operations  0.65 us (1%)
    pallas_call x1, Pallas kernels, factor_call(): pl.pallas_call(factor_kernel, out_shape=[jax.ShapeDtypeStruct((points, si...  22.4 us
    pallas_call x1, Pallas kernels, exchange(): pl.pallas_call(exchange_kernel, out_shape=[pltpu.VMEM((NC * HALF, 1, 128)...  22.3 us

profile of v2, /device:TPU:1, one launch (start us, length us, event | category | flops | bytes accessed | tf_op | source)
XLA Modules:
  0.0 45.4 jit_solution(9567793120368984303)
XLA Ops:
  0.6 0.0 copy-start
  0.6 22.3 %exchange.1 = (f32[768,1,128]{2,1,0:T(1,128)S(1)}, s32[2,256]{1,0:T(2,128)S(1)}) custom-call(s32[2,256]{1,0:T(2,128)} %piv_ref.1, f32[64,1024]{1,0:T(8,128)} %pts_ref.1), custom_call_target="tpu_custom_call" | custom-call | tf_op jit(solution)/shard_map/exchange/pallas_call | solution.py:156
  23.0 0.0 copy-done
  23.0 22.4 %factor.1 = (bf16[1024,512]{1,0:T(8,128)(2,1)}, f32[1,1024]{1,0:T(1,128)}) custom-call(s32[2,256]{1,0:T(2,128)S(1)} %get-tuple-element.6.place_ref, f32[768,1,128]{2,1,0:T(1,128)S(1)} %get-tuple-element.7.g_ref, f32[64,1024]{1,0:T(8,128)S(1)} %copy-done), custom_call_target="tpu_custom_call" | custom-call | tf_op jit(solution)/shard_map/factor/pallas_call | solution.py:360
Async XLA Ops:
  0.6 22.3 %copy-start = (f32[64,1024]{1,0:T(8,128)S(1)}, f32[64,1024]{1,0:T(8,128)}, u32[]{:S(2)}) copy-start(f32[64,1024]{1,0:T(8,128)} %pts_ref.1) | copy-start | bytes 786436

commit v3 on v2

--- a/solution.py
+++ b/solution.py
@@ -179,6 +179,9 @@
 LANES = 128
 HIGHEST = lax.Precision.HIGHEST
 CHUNK = 256
+GROUPS = 2
+LEAST = 20
+EARLY = 0
 
 
 def nt(left, right, precision=HIGHEST):
@@ -213,14 +216,6 @@
     norm_col = jnp.sum(squared, axis=1, keepdims=True)
     m_ref[...] = jnp.exp((norm_col + norm_row - 2.0 * nt(pivots, pivots)) * scale)
 
-    pts = pts_ref[...].T
-    norm_pts = jnp.sum(pts * pts, axis=1, keepdims=True)
-    kx = jnp.exp((norm_pts + norm_row - 2.0 * nt(pts, pivots)) * scale)
-    g_last_ref[...] = kx[:, size - LANES :]
-    kh, kl = halves(kx)
-    kh_ref[...] = kh
-    kl_ref[...] = kl
-
     sub = lax.broadcasted_iota(jnp.int32, (8, LANES), 0)
     lane = lax.broadcasted_iota(jnp.int32, (8, LANES), 1)
 
@@ -238,44 +233,83 @@
         start = blk * LANES
         part = [m_ref[start + 8 * g : start + 8 * g + 8, lanes(blk)] for g in range(LANES // 8)]
 
-        def update(g, off, own, turned):
-            factors = [spread(part[g][:, off + k : off + k + 1]) for k in range(8)]
-            new = jnp.where(own, 0.0, part[g])
-            for k in range(8):
-                new = new - factors[k] * turned[k]
-            part[g] = new
-
-        for g in range(len(part)):
-            off = 8 * g
-            rows = part[g]
-            cols = [spread(rows[:, off + k : off + k + 1]) for k in range(8)]
-            own = (lane >= off) & (lane < off + 8)
-            rows = jnp.where(own, jnp.where(lane - off == sub, 1.0, 0.0), rows)
-            kept = rows
-            diag = cols[0]
-            share = -(-len(trail) // 7)
-            bulk_share = -(-len(bulk) // ((len(part) - g) * 4))
-            for j in range(8):
-                inv = spread((1.0 / cols[j])[j : j + 1])
-                scaled = jnp.where(sub == j, 0.0, cols[j]) * inv
-                if j:
-                    diag = jnp.where(sub == j, cols[j], diag)
-                    kept = jnp.where(sub == j, rows, kept)
-                for k in range(j + 1, 8):
-                    cols[k] = cols[k] - scaled * spread(cols[k][j : j + 1])
-                rows = rows - scaled * spread(rows[j : j + 1])
-                pump(trail, share)
-                if j % 2:
-                    pump(bulk, bulk_share)
+        def factors_of(h, off):
+            return [spread(part[h][:, off + k : off + k + 1]) for k in range(8 * GROUPS)]
+
+        def update(h, off, own, turned, factors=None):
+            terms = [f * t for f, t in zip(factors or factors_of(h, off), turned)]
+            while len(terms) > 1:
+                terms = [p + q for p, q in zip(terms[::2], terms[1::2])]
+            part[h] = jnp.where(own, 0.0, part[h]) - terms[0]
+
+        def update_many(first, off, own, solved):
+            stack = jnp.concatenate(part[first:], axis=0)
+            change = nn(stack[:, off : off + 8 * GROUPS], solved)
+            for n in range(len(part) - first):
+                part[first + n] = jnp.where(own, 0.0, part[first + n]) - change[8 * n : 8 * n + 8]
+
+        count = len(part)
+        for g in range(0, count, GROUPS):
+            base = 8 * g
+            within = (lane >= base) & (lane < base + 8 * GROUPS)
+            some = range(GROUPS)
+            rows = [part[g + a] for a in some]
+            cols = [
+                [[spread(rows[a][:, base + 8 * b + k : base + 8 * b + k + 1]) for k in range(8)] for b in some]
+                for a in some
+            ]
+            turns = []
+            following = range(g + GROUPS, min(g + 2 * GROUPS, count))
+            for c in some:
+                off = base + 8 * c
+                own = (lane >= off) & (lane < off + 8)
+                eye = jnp.where(lane - off == sub, 1.0, 0.0)
+                rows = [jnp.where(own, eye if a == c else 0.0, rows[a]) for a in some]
+                share = -(-len(trail) // 4)
+                bulk_share = -(-len(bulk) // ((count - g - c) * 4))
+                if c == GROUPS - 1:
+                    pump(trail, len(trail))
+                    ready = {h: factors_of(h, base) for h in following}
+                for j in range(8):
+                    inv = spread((1.0 / cols[c][c][j])[j : j + 1])
+                    scaled = [
+                        (jnp.where(sub == j, 0.0, cols[a][c][j]) if a == c else cols[a][c][j]) * inv for a in some
+                    ]
+                    row = spread(rows[c][j : j + 1])
+                    if j:
+                        diag = jnp.where(sub == j, cols[c][c][j], diag)
+                        turn = jnp.where(sub == j, inv, turn)
+                        kept = jnp.where(sub == j, rows[c], kept)
+                    else:
+                        diag, turn, kept = cols[c][c][j], inv, rows[c]
+                    for b in range(c, GROUPS):
+                        for k in range(j + 1 if b == c else 0, 8):
+                            value = spread(cols[c][b][k][j : j + 1])
+                            for a in some:
+                                cols[a][b][k] = cols[a][b][k] - scaled[a] * value
+                    rows = [r - f * row for r, f in zip(rows, scaled)]
+                    pump(trail, share)
+                    if j % 2:
+                        pump(bulk, bulk_share)
+                turns.append(turn)
+                kept = jnp.where(lane < off + 8, kept, 0.0) * lax.rsqrt(diag)
+                s_ref[start + off : start + off + 8, lanes(blk)] = kept
             pump(trail, len(trail))
-            rows = rows * (1.0 / diag)
-            turned = [spread(rows[k : k + 1]) for k in range(8)]
-            kept = jnp.where(lane < off + 8, kept, 0.0) * lax.rsqrt(diag)
-            s_ref[start + off : start + off + 8, lanes(blk)] = kept
-            if g + 1 < len(part):
-                update(g + 1, off, own, turned)
-            for h in range(g + 2, len(part)):
-                trail.append(lambda h=h, off=off, own=own, turned=turned: update(h, off, own, turned))
+            solved = [r * t for r, t in zip(rows, turns)]
+            turned = [spread(t[k : k + 1]) for t in solved for k in range(8)]
+            for h in following:
+                update(h, base, within, turned, ready[h])
+            first = g + 2 * GROUPS
+            stop = min(count, g + 3 * GROUPS)
+            if count - stop <= LEAST:
+                stop = count
+            for h in range(first, stop):
+                trail.append(lambda h=h, base=base, within=within, turned=turned: update(h, base, within, turned))
+            if stop < count:
+                together = jnp.concatenate(solved, axis=0)
+                trail.append(
+                    lambda stop=stop, base=base, within=within, together=together: update_many(stop, base, within, together)
+                )
         pump(bulk, len(bulk))
 
     def block(ref, r, c):
@@ -291,6 +325,16 @@
         change = nn(l_ref[r * LANES : (r + 1) * LANES, :], block(s_ref, blk, c))
         old = 0.0 if c == blk else block(m_ref, r, c)
         m_ref[r * LANES : (r + 1) * LANES, lanes(c)] = old - change
+
+    def put_kernel(r0):
+        part = slice(r0, r0 + CHUNK)
+        pts = pts_ref[:, part].T
+        norm_pts = jnp.sum(pts * pts, axis=1, keepdims=True)
+        kx = jnp.exp((norm_pts + norm_row - 2.0 * nt(pts, pivots)) * scale)
+        g_last_ref[part, :] = kx[:, size - LANES :]
+        high, low = halves(kx)
+        kh_ref[part, :] = high
+        kl_ref[part, :] = low
 
     def finish(new, part, c):
         f_ref[part, lanes(c)] = new.astype(jnp.bfloat16)
@@ -321,6 +365,10 @@
         kh_ref[part, lanes(last)] = high
         kl_ref[part, lanes(last)] = low
 
+    for r0 in range(0, points, CHUNK):
+        bulk.append(lambda r0=r0: put_kernel(r0))
+    if EARLY:
+        pump(bulk, len(bulk))
     for blk in range(wide):
         diagonal(blk)
         if blk == last:

time: 45.5 us -> 41.6 us (0.914)
  Pallas kernels: 44.7 us -> 40.8 us
    pallas_call x1, Pallas kernels: 22.4 us -> 18.5 us  [factor_call(): pl.pallas_call(factor_kernel, out_shape=[jax.ShapeDtypeStruct((points, si...]
where the time goes in v3:
time: 41.6 us; the launch traced here: 41.4 us
  Pallas kernels  40.8 us (98%)
  between operations  0.65 us (2%)
    pallas_call x1, Pallas kernels, exchange(): pl.pallas_call(exchange_kernel, out_shape=[pltpu.VMEM((NC * HALF, 1, 128)...  22.3 us
    pallas_call x1, Pallas kernels, factor_call(): pl.pallas_call(factor_kernel, out_shape=[jax.ShapeDtypeStruct((points, si...  18.5 us

profile of v3, /device:TPU:1, one launch (start us, length us, event | category | flops | bytes accessed | tf_op | source)
XLA Modules:
  0.0 41.4 jit_solution(6342785285552320026)
XLA Ops:
  0.6 0.0 copy-start
  0.6 22.3 %exchange.1 = (f32[768,1,128]{2,1,0:T(1,128)S(1)}, s32[2,256]{1,0:T(2,128)S(1)}) custom-call(s32[2,256]{1,0:T(2,128)} %piv_ref.1, f32[64,1024]{1,0:T(8,128)} %pts_ref.1), custom_call_target="tpu_custom_call" | custom-call | tf_op jit(solution)/shard_map/exchange/pallas_call | solution.py:156
  23.0 0.0 copy-done
  23.0 18.5 %factor.1 = (bf16[1024,512]{1,0:T(8,128)(2,1)}, f32[1,1024]{1,0:T(1,128)}) custom-call(s32[2,256]{1,0:T(2,128)S(1)} %get-tuple-element.6.place_ref, f32[768,1,128]{2,1,0:T(1,128)S(1)} %get-tuple-element.7.g_ref, f32[64,1024]{1,0:T(8,128)S(1)} %copy-done), custom_call_target="tpu_custom_call" | custom-call | tf_op jit(solution)/shard_map/factor/pallas_call | solution.py:408
Async XLA Ops:
  0.6 22.3 %copy-start = (f32[64,1024]{1,0:T(8,128)S(1)}, f32[64,1024]{1,0:T(8,128)}, u32[]{:S(2)}) copy-start(f32[64,1024]{1,0:T(8,128)} %pts_ref.1) | copy-start | bytes 786436

commit v4 on v3

--- a/solution.py
+++ b/solution.py
@@ -27,7 +27,8 @@
     def z_peer(k):
         return device(x, y, lax.rem(z + k, NZ), core)
 
-    flat = [(i, k) for i in range(NX) for k in range(NY) if i or k]
+    flat = [(2, 2), (2, 1), (1, 2), (2, 3), (3, 2), (1, 1), (3, 3), (1, 3), (3, 1)]
+    flat += [(0, 2), (2, 0), (0, 1), (1, 0), (0, 3), (3, 0)]
 
     def plane_peer(i, k):
         return device(lax.rem(x + i, NX), lax.rem(y + k, NY), z, core)

time: 41.6 us -> 41.3 us (level)
  no operation moved by 1% of the time
where the time goes in v4:
time: 41.3 us; the launch traced here: 41.2 us
  Pallas kernels  40.5 us (98%)
  between operations  0.65 us (2%)
    pallas_call x1, Pallas kernels, exchange(): pl.pallas_call(exchange_kernel, out_shape=[pltpu.VMEM((NC * HALF, 1, 128)...  22 us
    pallas_call x1, Pallas kernels, factor_call(): pl.pallas_call(factor_kernel, out_shape=[jax.ShapeDtypeStruct((points, si...  18.5 us

profile of v4, /device:TPU:1, one launch (start us, length us, event | category | flops | bytes accessed | tf_op | source)
XLA Modules:
  0.0 41.2 jit_solution(13157685101424025919)
XLA Ops:
  0.6 0.0 copy-start
  0.6 22.0 %exchange.1 = (f32[768,1,128]{2,1,0:T(1,128)S(1)}, s32[2,256]{1,0:T(2,128)S(1)}) custom-call(s32[2,256]{1,0:T(2,128)} %piv_ref.1, f32[64,1024]{1,0:T(8,128)} %pts_ref.1), custom_call_target="tpu_custom_call" | custom-call | tf_op jit(solution)/shard_map/exchange/pallas_call | solution.py:157
  22.7 0.0 copy-done
  22.7 18.5 %factor.1 = (bf16[1024,512]{1,0:T(8,128)(2,1)}, f32[1,1024]{1,0:T(1,128)}) custom-call(s32[2,256]{1,0:T(2,128)S(1)} %get-tuple-element.6.place_ref, f32[768,1,128]{2,1,0:T(1,128)S(1)} %get-tuple-element.7.g_ref, f32[64,1024]{1,0:T(8,128)S(1)} %copy-done), custom_call_target="tpu_custom_call" | custom-call | tf_op jit(solution)/shard_map/factor/pallas_call | solution.py:409
Async XLA Ops:
  0.6 22.1 %copy-start = (f32[64,1024]{1,0:T(8,128)S(1)}, f32[64,1024]{1,0:T(8,128)}, u32[]{:S(2)}) copy-start(f32[64,1024]{1,0:T(8,128)} %pts_ref.1) | copy-start | bytes 786436
